TPU v7x, 32 devices: a whole 2x2x4 slice. The times are simulated.
32 devices in a mesh: grp: 4 (over y, x), dev: 8 (over z, core).
Axes of the slice: x: 2, y: 2, z: 4, core: 2. Of those that a mesh axis runs over, the one named last changes fastest.
Arguments:
- points: float32 [64, 49152], P(None, 'dev'), may hold values from -6 to 6
- weights: float32 [49152, 128], P('dev'), may hold values from -4 to 4
- proj: float32 [256, 49152], P(None, 'dev'), may hold values from -0.078125 to 0.078125
- fetch_table: int32 [3, 8, 8, 2], P(None, 'dev'), may hold values from 0 to 11, as said below
- near_list: int32 [96, 16], P('dev'), may hold values from 0 to 15, as said below
- far_list: int32 [96, 8], P('dev'), may hold values from 0 to 7, as said below
- skel_idx: int32 [8, 256], P('dev'), may hold values from 0 to 6143, as said below
Outputs:
- potential: float32 [49152, 128], P('dev')
Inputs may be any that keep to these rules, and one draw needn't show every extreme that they name: Entries of fetch_table[r, d, e] are distinct local leaf numbers of column e. `near_list`: the 16 slots of one target leaf are distinct. `far_list`: the 8 nodes of one target leaf are distinct, and one of them is node (c + 1) mod 8 for the leaf's column c. `skel_idx`: the 256 skeleton points of one node are distinct.
All inputs are finite; a program needn't handle non-finite values.
Results may differ from a plain program's by a relative error of at most 0.0003.
Values sent between devices are 32-bit elements; how exact they have to be, the bound alone decides.
No kernel may reach another device: no remote copies, remote signals or barrier semaphores. Data moves between devices by JAX's collectives and lax.ppermute only.
A program may use at most 192 MiB of HBM per device.

v0:
```python
import jax
import jax.numpy as jnp
from jax import lax
from jax.sharding import PartitionSpec as P


def kernel_sum(target, sources, values):
    high = lax.Precision.HIGHEST
    inner = jnp.einsum("dt,jds->tjs", target, sources, precision=high)
    target_norm = jnp.sum(target * target, axis=0)
    source_norm = jnp.sum(sources * sources, axis=1)
    distance = target_norm[:, None, None] + source_norm[None] - 2.0 * inner
    kernel = jnp.exp(-distance * (2.0 / target.shape[0]))
    return jnp.einsum("tjs,jsw->tw", kernel, values, precision=high)


def on_device(points, weights, proj, fetch_table, near_list, far_list, skel_idx):
    features, column_points = points.shape
    columns = weights.shape[1]
    devices = lax.axis_size("dev")
    groups = lax.axis_size("grp")
    targets = near_list.shape[0]
    leaf_size = column_points // targets
    row_leaves = targets // (groups - 1)
    capacity = fetch_table.shape[3]
    group_index = lax.axis_index("grp")
    near_row = jnp.minimum(group_index, groups - 2)
    far_side = group_index == groups - 1
    leaf_coords = points.reshape(features, targets, leaf_size)
    leaf_weights = weights.reshape(targets, leaf_size, columns)
    requests = lax.dynamic_index_in_dim(fetch_table[:, 0], near_row, 0, keepdims=False)
    asked = lax.all_to_all(requests, "dev", split_axis=0, concat_axis=0, tiled=True)
    coords = jnp.moveaxis(jnp.take(leaf_coords, asked, axis=1), 0, 2)
    values = jnp.take(leaf_weights, asked, axis=0)
    fetched_coords = lax.all_to_all(coords, "dev", split_axis=0, concat_axis=0, tiled=True)
    fetched_values = lax.all_to_all(values, "dev", split_axis=0, concat_axis=0, tiled=True)
    flat_coords = fetched_coords.reshape(devices * capacity, features, leaf_size)
    flat_values = fetched_values.reshape(devices * capacity, leaf_size, columns)
    local_skeleton = jnp.take(points, skel_idx[0], axis=1)
    share_len = column_points // groups
    share_start = group_index * share_len
    share_proj = lax.dynamic_slice_in_dim(proj, share_start, share_len, 1)
    share_weights = lax.dynamic_slice_in_dim(weights, share_start, share_len, 0)
    partial_value = jnp.dot(
        share_proj,
        share_weights,
        preferred_element_type=jnp.float32,
        precision=lax.Precision.HIGHEST,
    )
    node_weights = lax.psum(partial_value, "grp")
    skel_coords, skel_weights = (
        lax.all_gather(local_skeleton[None], "dev", axis=0, tiled=True),
        lax.all_gather(node_weights[None], "dev", axis=0, tiled=True),
    )

    def near_work():
        slots = lax.dynamic_slice_in_dim(near_list, near_row * row_leaves, row_leaves, 0)
        leaf_numbers = near_row * row_leaves + jnp.arange(row_leaves, dtype=jnp.int32)

        def near_leaf(items):
            leaf_number, leaf_slots = items
            target = jnp.take(leaf_coords, leaf_number, axis=1)
            return kernel_sum(
                target,
                jnp.take(flat_coords, leaf_slots, axis=0),
                jnp.take(flat_values, leaf_slots, axis=0),
            )

        block = lax.map(near_leaf, (leaf_numbers, slots))
        empty = jnp.zeros((targets, leaf_size, columns), jnp.float32)
        return lax.dynamic_update_slice_in_dim(empty, block, near_row * row_leaves, 0)

    def far_work():

        def far_leaf(items):
            leaf_number, node_ids = items
            target = jnp.take(leaf_coords, leaf_number, axis=1)
            return kernel_sum(
                target,
                jnp.take(skel_coords, node_ids, axis=0),
                jnp.take(skel_weights, node_ids, axis=0),
            )

        return lax.map(far_leaf, (jnp.arange(targets, dtype=jnp.int32), far_list))

    contribution = lax.cond(far_side, far_work, near_work)
    total = lax.psum(contribution, "grp")
    return total.reshape(column_points, columns)


def solution(mesh):
    placed = (
        P(None, "dev"),
        P("dev", None),
        P(None, "dev"),
        P(None, "dev", None, None),
        P("dev", None),
        P("dev", None),
        P("dev", None),
    )
    return jax.shard_map(
        on_device, mesh=mesh, in_specs=placed, out_specs=P("dev", None), check_vma=False
    )
```

profile of v0, /device:TPU:0, one launch (start us, length us, event | category | flops | bytes accessed | tf_op | source)
XLA Modules:
  0.0 515.7 jit_solution(13828682134783458848)
XLA Ops:
  6.5 0.8 dynamic-slice_bitcast_fusion
  7.4 0.7 copy.24
  8.0 6.4 %all-to-all-start = ((s32[8,1,2]{2,1,0:T(1,128)}), s32[8,1,2]{2,1,0:T(1,128)S(1)}, u32[]{:S(2)}, u32[]{:S(2)}) async-start(s32[8,1,2]{2,1,0:T(1,128)} %copy.24), calls=%async_computation | async-start | bytes 8192 | tf_op jit(solution)/shard_map/all_to_all | solution.py:32
  14.4 2.7 copy.52
  17.1 2.8 all-to-all-done
  20.3 3.4 gather_fusion.4
  23.7 3.3 broadcast_select_fusion.1
  27.0 4.4 all-to-all-start.1
  31.4 2.8 gather_fusion.5
  34.2 4.6 broadcast_select_fusion
  38.8 41.6 %all-to-all-done.1 = f32[8,2,64,512]{3,2,1,0:T(8,128)} async-done(((f32[8,2,64,512]{3,2,1,0:T(8,128)}), f32[8,2,64,512]{3,2,1,0:T(8,128)}, u32[]{:S(2)}, u32[]{:S(2)}) %all-to-all-start.1) | async-done | bytes 2097184 | tf_op jit(solution)/shard_map/all_to_all | solution.py:35
  80.4 4.6 all-to-all-start.2
  85.0 3.5 fusion.72
  88.6 43.7 %all-reduce.3.cloned.1.call-done = f32[1,256,128]{2,1,0:T(8,128)} async-done(((f32[1,256,128]{2,1,0:T(8,128)}), f32[1,256,128]{2,1,0:T(8,128)}) %all-reduce.3.cloned.1.call-update) | async-done | bytes 131088 | tf_op jit(solution)/shard_map/psum | solution.py:50
  132.4 2.9 reshape.190
  135.2 2.3 copy.31
  137.5 2.6 gather_fusion.6
  140.3 56.1 %all_gather.6 = f32[8,64,256]{2,1,0:T(8,128)} all-gather(f32[1,64,256]{2,1,0:T(8,128)S(1)} %copy.32), channel_id=1, replica_groups=mesh['grp'=4,'dev'=8] {'dev'}, dimensions={0}, use_global_device_ids=true | all-gather | bytes 589824 | tf_op jit(solution)/shard_map/all_gather | solution.py:52
  196.5 202.2 %conditional.1 = (f32[12,512,128]{2,1,0:T(8,128)}) conditional(s32[]{:T(128)} %convert_element_type.3, (s32[]{:T(128)}, s32[12,16]{1,0:T(8,128)}, f32[8,2,64,512]{3,2,1,0:T(8,128)}, f32[8,2,512,128]{3,2,1,0:T(8,128)}, f32[64,12,512]{2,1,0:T(8,128)}) %tuple.20, (f32[64,12,512]{2,1,0:T(8,128)}, s32[12,8]{0,1:T(8,128)S(1)}, f32[8,64,256]{2,1,0:T(8,128)}, ...), branch_computations={%region_1.7_spmd, %region_6.12_spmd} | conditional | flops 9687917568 | bytes 60630836 | solution.py:86
  196.5 0.7 constant_dynamic-slice_fusion.2
  197.2 197.3 %while.19 = (s32[]{:T(128)}, f32[4,512,128]{2,1,0:T(8,128)}, s32[4]{0:T(128)S(1)}, f32[64,12,512]{2,1,0:T(8,128)}, s32[4,16]{1,0:T(4,128)S(1)}, /*index=5*/f32[1...) while((s32[]{:T(128)}, f32[4,512,128]{2,1,0:T(8,128)}, ...), condition=%wide.region_5.6_spmd, body=%wide.region_2.5_spmd.sunk | while | flops 9687917568 | bytes 55387260 | solution.py:69
  197.2 0.6 dynamic_slice.61
  199.7 1.3 constant_dynamic-slice_fusion.8
  201.1 2.3 gather_fusion.3
  203.4 16.2 %fusion.106 = f32[512,16,512]{2,0,1:T(8,128)} fusion(f32[16,64,512]{2,1,0:T(8,128)S(1)} %gather_fusion.3, pred[16]{0:T(512)(128)(4,1)S(1)} %compare_and_fusion.7, f32[64,1,512]{2,1,0:T(1,128)S(1)} %constant_dynamic-slice_fusion.8, pred[]{:T(512)S(6)} %and.56), kind=kOutput, calls=%fused_computation.22.clone.1 | convolution fusion | flops 3221782528 | bytes 19005456 | tf_op jit(solution)/shard_map/cond/branch_0_fun/while/body/eval_jaxpr/dt,jds->tjs/dot_general | solution.py:9
  220.0 5.0 gather_fusion.2
  225.0 21.5 %fusion.108 = f32[4,512,128]{2,1,0:T(8,128)} fusion(f32[4,512,128]{2,1,0:T(8,128)} %get-tuple-element.303, s32[]{:T(128)} %get-tuple-element.302, f32[16,512,128]{2,1,0:T(8,128)} %gather_fusion.2, pred[16]{0:T(512)(128)(4,1)S(1)} %compare_and_fusion.7, f32[512,16,512]{2,0,1:T(8,128)} %fusion.106, f32[16,512]{1,0:T(8,128)S(1)} %multiply_reduce_fusion.5, ...), kind=kOutput, calls=%fused_computation.25.clone.1 | convolution fusion | flops 6464471040 | bytes 21269008 | tf_op jit(solution)/shard_map/cond/branch_0_fun/while/body/eval_jaxpr/tjs,jsw->tw/dot_general | solution.py:14
  246.5 0.6 dynamic_slice.61
  249.0 1.3 constant_dynamic-slice_fusion.8
  250.4 2.3 gather_fusion.3
  252.7 16.2 %fusion.106 = f32[512,16,512]{2,0,1:T(8,128)} fusion(f32[16,64,512]{2,1,0:T(8,128)S(1)} %gather_fusion.3, pred[16]{0:T(512)(128)(4,1)S(1)} %compare_and_fusion.7, f32[64,1,512]{2,1,0:T(1,128)S(1)} %constant_dynamic-slice_fusion.8, pred[]{:T(512)S(6)} %and.56), kind=kOutput, calls=%fused_computation.22.clone.1 | convolution fusion | flops 3221782528 | bytes 19005456 | tf_op jit(solution)/shard_map/cond/branch_0_fun/while/body/eval_jaxpr/dt,jds->tjs/dot_general | solution.py:9
  269.3 5.0 gather_fusion.2
  274.3 21.5 %fusion.108 = f32[4,512,128]{2,1,0:T(8,128)} fusion(f32[4,512,128]{2,1,0:T(8,128)} %get-tuple-element.303, s32[]{:T(128)} %get-tuple-element.302, f32[16,512,128]{2,1,0:T(8,128)} %gather_fusion.2, pred[16]{0:T(512)(128)(4,1)S(1)} %compare_and_fusion.7, f32[512,16,512]{2,0,1:T(8,128)} %fusion.106, f32[16,512]{1,0:T(8,128)S(1)} %multiply_reduce_fusion.5, ...), kind=kOutput, calls=%fused_computation.25.clone.1 | convolution fusion | flops 6464471040 | bytes 21269008 | tf_op jit(solution)/shard_map/cond/branch_0_fun/while/body/eval_jaxpr/tjs,jsw->tw/dot_general | solution.py:14
  298.4 1.3 constant_dynamic-slice_fusion.8
  299.8 2.3 gather_fusion.3
  302.1 16.2 %fusion.106 = f32[512,16,512]{2,0,1:T(8,128)} fusion(f32[16,64,512]{2,1,0:T(8,128)S(1)} %gather_fusion.3, pred[16]{0:T(512)(128)(4,1)S(1)} %compare_and_fusion.7, f32[64,1,512]{2,1,0:T(1,128)S(1)} %constant_dynamic-slice_fusion.8, pred[]{:T(512)S(6)} %and.56), kind=kOutput, calls=%fused_computation.22.clone.1 | convolution fusion | flops 3221782528 | bytes 19005456 | tf_op jit(solution)/shard_map/cond/branch_0_fun/while/body/eval_jaxpr/dt,jds->tjs/dot_general | solution.py:9
  318.6 5.0 gather_fusion.2
  323.6 21.5 %fusion.108 = f32[4,512,128]{2,1,0:T(8,128)} fusion(f32[4,512,128]{2,1,0:T(8,128)} %get-tuple-element.303, s32[]{:T(128)} %get-tuple-element.302, f32[16,512,128]{2,1,0:T(8,128)} %gather_fusion.2, pred[16]{0:T(512)(128)(4,1)S(1)} %compare_and_fusion.7, f32[512,16,512]{2,0,1:T(8,128)} %fusion.106, f32[16,512]{1,0:T(8,128)S(1)} %multiply_reduce_fusion.5, ...), kind=kOutput, calls=%fused_computation.25.clone.1 | convolution fusion | flops 6464471040 | bytes 21269008 | tf_op jit(solution)/shard_map/cond/branch_0_fun/while/body/eval_jaxpr/tjs,jsw->tw/dot_general | solution.py:14
  345.1 0.6 dynamic_slice.61
  347.7 1.3 constant_dynamic-slice_fusion.8
  349.1 2.3 gather_fusion.3
  351.4 16.2 %fusion.106 = f32[512,16,512]{2,0,1:T(8,128)} fusion(f32[16,64,512]{2,1,0:T(8,128)S(1)} %gather_fusion.3, pred[16]{0:T(512)(128)(4,1)S(1)} %compare_and_fusion.7, f32[64,1,512]{2,1,0:T(1,128)S(1)} %constant_dynamic-slice_fusion.8, pred[]{:T(512)S(6)} %and.56), kind=kOutput, calls=%fused_computation.22.clone.1 | convolution fusion | flops 3221782528 | bytes 19005456 | tf_op jit(solution)/shard_map/cond/branch_0_fun/while/body/eval_jaxpr/dt,jds->tjs/dot_general | solution.py:9
  367.9 5.0 gather_fusion.2
  372.9 21.5 %fusion.108 = f32[4,512,128]{2,1,0:T(8,128)} fusion(f32[4,512,128]{2,1,0:T(8,128)} %get-tuple-element.303, s32[]{:T(128)} %get-tuple-element.302, f32[16,512,128]{2,1,0:T(8,128)} %gather_fusion.2, pred[16]{0:T(512)(128)(4,1)S(1)} %compare_and_fusion.7, f32[512,16,512]{2,0,1:T(8,128)} %fusion.106, f32[16,512]{1,0:T(8,128)S(1)} %multiply_reduce_fusion.5, ...), kind=kOutput, calls=%fused_computation.25.clone.1 | convolution fusion | flops 6464471040 | bytes 21269008 | tf_op jit(solution)/shard_map/cond/branch_0_fun/while/body/eval_jaxpr/tjs,jsw->tw/dot_general | solution.py:14
  394.5 2.0 broadcast.199
  396.4 2.3 constant_dynamic-update-slice_fusion
  398.7 106.7 %all-reduce.5.cloned.1.call-done = f32[6144,128]{1,0:T(8,128)} async-done(((f32[6144,128]{1,0:T(8,128)}), f32[6144,128]{1,0:T(8,128)}) %all-reduce.5.cloned.1.call-update) | async-done | bytes 3145744 | tf_op jit(solution)/shard_map/psum | solution.py:87
  505.4 3.8 copy.80
  (53 shorter events, 3.2 us)
Async XLA Ops:
  6.5 24.8 %copy-start = (f32[6144,128]{1,0:T(8,128)S(1)}, f32[6144,128]{1,0:T(8,128)}, u32[]{:S(2)}) copy-start(f32[6144,128]{1,0:T(8,128)} %param.16) | copy-start | bytes 9437188
  8.0 11.9 %all-to-all-start = ((s32[8,1,2]{2,1,0:T(1,128)}), s32[8,1,2]{2,1,0:T(1,128)S(1)}, u32[]{:S(2)}, u32[]{:S(2)}) async-start(s32[8,1,2]{2,1,0:T(1,128)} %copy.24), calls=%async_computation | async-start | bytes 8192 | tf_op jit(solution)/shard_map/all_to_all | solution.py:32
  27.0 53.4 %all-to-all-start.1 = ((f32[8,2,64,512]{3,2,1,0:T(8,128)}), f32[8,2,64,512]{3,2,1,0:T(8,128)}, u32[]{:S(2)}, u32[]{:S(2)}) async-start(f32[8,2,64,512]{3,2,1,0:T(8,128)} %broadcast_select_fusion.1), calls=%async_computation.1 | async-start | bytes 4194304 | tf_op jit(solution)/shard_map/all_to_all | solution.py:35
  80.4 116.1 %all-to-all-start.2 = ((f32[8,2,512,128]{3,2,1,0:T(8,128)}), f32[8,2,512,128]{3,2,1,0:T(8,128)}, u32[]{:S(2)}, u32[]{:S(2)}) async-start(f32[8,2,512,128]{3,2,1,0:T(8,128)} %broadcast_select_fusion), calls=%async_computation.2 | async-start | bytes 8388608 | tf_op jit(solution)/shard_map/all_to_all | solution.py:36
  85.0 47.3 %all-reduce.3.cloned.1.call-start = ((), (), s32[]{:S(2)}) async-start(), calls=%async_computation.3 | async-start | bytes 262144 | tf_op jit(solution)/shard_map/psum | solution.py:50
  88.5 46.7 %copy-start.3 = (f32[64,6144]{1,0:T(8,128)S(1)}, f32[64,6144]{1,0:T(8,128)}, u32[]{:S(2)}) copy-start(f32[64,6144]{1,0:T(8,128)} %param.15) | copy-start | bytes 4718596
  88.5 107.9 %all-gather.2.cloned.1.call-start = ((), (), s32[]{:S(2)}) async-start(), calls=%async_computation.4 | async-start | bytes 1179648 | tf_op jit(solution)/shard_map/all_gather | solution.py:53
  132.3 5.2 %copy-start.5 = (s32[1,256]{1,0:T(1,128)S(1)}, s32[1,256]{1,0:T(1,128)}, u32[]{:S(2)}) copy-start(s32[1,256]{1,0:T(1,128)} %param.21) | copy-start | bytes 3076
  132.3 64.1 %copy-start.4 = (s32[12,8]{0,1:T(8,128)S(1)}, s32[12,8]{0,1:T(8,128)}, u32[]{:S(2)}) copy-start(s32[12,8]{0,1:T(8,128)} %param.20) | copy-start | bytes 1156
  132.3 373.1 %all-reduce.5.cloned.1.call-start = ((), (), s32[]{:S(2)}) async-start(), calls=%async_computation.5 | async-start | bytes 6291456 | tf_op jit(solution)/shard_map/psum | solution.py:87
  398.7 110.5 %copy-start.1 = (f32[6144,128]{1,0:T(8,128)S(1)}, f32[6144,128]{1,0:T(8,128)}, u32[]{:S(2)}) copy-start(f32[6144,128]{1,0:T(8,128)} %param.16) | copy-start | bytes 9437188
Sparse Core Ops, SparseCore 0:
  88.7 43.5 all-reduce.2
  133.9 39.0 all-gather.1
  398.8 106.5 all-reduce.4
where the time goes:
time: 518 us; the launch traced here: 516 us
  waiting for transfers between devices  195 us (38%)
  matrix products  154 us (30%)
  local copies, waits for them, and re-layouts  64.2 us (12%)
  blocking collectives  56.1 us (11%)
  starting transfers between devices  15.4 us (3%)
  between operations  13.2 us (3%)
  other arithmetic  9.78 us (2%)
  loops' own time  7.83 us (2%)
    psum x1, waiting for transfers between devices, on_device(): total = lax.psum(contribution, 'grp')  107 us
    dot_general x4, matrix products, kernel_sum(): return jnp.einsum('tjs,jsw->tw', kernel, values, precision=high)  86.1 us
    dot_general x4, matrix products, kernel_sum(): inner = jnp.einsum('dt,jds->tjs', target, sources, precision=high)  64.6 us
    all_gather x1, blocking collectives, on_device(): lax.all_gather(local_skeleton[None], 'dev', axis=0, tiled=True)  56.1 us
    psum x1, waiting for transfers between devices, on_device(): node_weights = lax.psum(partial_value, 'grp')  43.7 us
    all_to_all x1, waiting for transfers between devices, on_device(): lax.all_to_all(coords, 'dev', split_axis=0, concat_axis=0, tiled=True)  41.6 us
    gather x4, local copies, waits for them, and re-layouts, near_leaf(): jnp.take(flat_values, leaf_slots, axis=0)  19.9 us
  transfers between devices with their start and end apart: 6, of which 4 were waited for; matrix products, arithmetic and copies ran while one was open for 4% of the time, Pallas kernels for 0%

commit v1 on v0

--- a/solution.py
+++ b/solution.py
@@ -84,7 +84,8 @@
         return lax.map(far_leaf, (jnp.arange(targets, dtype=jnp.int32), far_list))
 
     contribution = lax.cond(far_side, far_work, near_work)
-    total = lax.psum(contribution, "grp")
+    shards = lax.all_gather(contribution, "grp", axis=0, tiled=False)
+    total = shards.sum(axis=0)
     return total.reshape(column_points, columns)
 
 

time: 518 us -> 557 us (1.075)
  waiting for transfers between devices: 195 us -> 230 us
  other arithmetic: 9.78 us -> 17.3 us
    all_gather x0 -> x1, waiting for transfers between devices: none -> 142 us  [on_device(): shards = lax.all_gather(contribution, 'grp', axis=0, tiled=False)]
    psum x1 -> x0, waiting for transfers between devices: 107 us -> none  [on_device(): total = lax.psum(contribution, 'grp')]
    reduce_sum x0 -> x1, other arithmetic: none -> 7.56 us  [on_device(): total = shards.sum(axis=0)]
where the time goes in v1:
time: 557 us; the launch traced here: 555 us
  waiting for transfers between devices  230 us (41%)
  matrix products  154 us (28%)
  local copies, waits for them, and re-layouts  60.5 us (11%)
  blocking collectives  56.1 us (10%)
  other arithmetic  17.3 us (3%)
  starting transfers between devices  15.4 us (3%)
  between operations  13.2 us (2%)
  loops' own time  7.83 us (1%)
    all_gather x1, waiting for transfers between devices, on_device(): shards = lax.all_gather(contribution, 'grp', axis=0, tiled=False)  142 us
    dot_general x4, matrix products, kernel_sum(): return jnp.einsum('tjs,jsw->tw', kernel, values, precision=high)  86.1 us
    dot_general x4, matrix products, kernel_sum(): inner = jnp.einsum('dt,jds->tjs', target, sources, precision=high)  64.6 us
    all_gather x1, blocking collectives, on_device(): lax.all_gather(local_skeleton[None], 'dev', axis=0, tiled=True)  56.1 us
    psum x1, waiting for transfers between devices, on_device(): node_weights = lax.psum(partial_value, 'grp')  43.7 us
    all_to_all x1, waiting for transfers between devices, on_device(): lax.all_to_all(coords, 'dev', split_axis=0, concat_axis=0, tiled=True)  41.6 us
    gather x4, local copies, waits for them, and re-layouts, near_leaf(): jnp.take(flat_values, leaf_slots, axis=0)  19.9 us
  transfers between devices with their start and end apart: 6, of which 4 were waited for; matrix products, arithmetic and copies ran while one was open for 4% of the time, Pallas kernels for 0%

profile of v1, /device:TPU:0, one launch (start us, length us, event | category | flops | bytes accessed | tf_op | source)
XLA Modules:
  0.0 554.9 jit_solution(18411011494372701988)
XLA Ops:
  6.5 0.8 dynamic-slice_bitcast_fusion
  7.4 0.7 copy.24
  8.0 6.4 %all-to-all-start = ((s32[8,1,2]{2,1,0:T(1,128)}), s32[8,1,2]{2,1,0:T(1,128)S(1)}, u32[]{:S(2)}, u32[]{:S(2)}) async-start(s32[8,1,2]{2,1,0:T(1,128)} %copy.24), calls=%async_computation | async-start | bytes 8192 | tf_op jit(solution)/shard_map/all_to_all | solution.py:32
  14.4 2.7 copy.52
  17.1 2.8 all-to-all-done
  20.3 3.4 gather_fusion.4
  23.7 3.3 broadcast_select_fusion.1
  27.0 4.4 all-to-all-start.1
  31.4 2.8 gather_fusion.5
  34.2 4.6 broadcast_select_fusion
  38.8 41.6 %all-to-all-done.1 = f32[8,2,64,512]{3,2,1,0:T(8,128)} async-done(((f32[8,2,64,512]{3,2,1,0:T(8,128)}), f32[8,2,64,512]{3,2,1,0:T(8,128)}, u32[]{:S(2)}, u32[]{:S(2)}) %all-to-all-start.1) | async-done | bytes 2097184 | tf_op jit(solution)/shard_map/all_to_all | solution.py:35
  80.4 4.6 all-to-all-start.2
  85.0 3.5 fusion.72
  88.6 43.7 %all-reduce.2.cloned.1.call-done = f32[1,256,128]{2,1,0:T(8,128)} async-done(((f32[1,256,128]{2,1,0:T(8,128)}), f32[1,256,128]{2,1,0:T(8,128)}) %all-reduce.2.cloned.1.call-update) | async-done | bytes 131088 | tf_op jit(solution)/shard_map/psum | solution.py:50
  132.4 2.9 reshape.190
  135.2 2.3 copy.31
  137.5 2.6 gather_fusion.6
  140.3 56.1 %all_gather.12 = f32[8,64,256]{2,1,0:T(8,128)} all-gather(f32[1,64,256]{2,1,0:T(8,128)S(1)} %copy.32), channel_id=1, replica_groups=mesh['grp'=4,'dev'=8] {'dev'}, dimensions={0}, use_global_device_ids=true | all-gather | bytes 589824 | tf_op jit(solution)/shard_map/all_gather | solution.py:52
  196.5 202.2 %conditional.1 = (f32[12,512,128]{2,1,0:T(8,128)}) conditional(s32[]{:T(128)} %convert_element_type.3, (s32[]{:T(128)}, s32[12,16]{1,0:T(8,128)}, f32[8,2,64,512]{3,2,1,0:T(8,128)}, f32[8,2,512,128]{3,2,1,0:T(8,128)}, f32[64,12,512]{2,1,0:T(8,128)}) %tuple.20, (f32[64,12,512]{2,1,0:T(8,128)}, s32[12,8]{0,1:T(8,128)S(1)}, f32[8,64,256]{2,1,0:T(8,128)}, ...), branch_computations={%region_1.7_spmd, %region_6.12_spmd} | conditional | flops 9687917568 | bytes 60630836 | solution.py:86
  196.5 0.7 constant_dynamic-slice_fusion.2
  197.2 197.3 %while.19 = (s32[]{:T(128)}, f32[4,512,128]{2,1,0:T(8,128)}, s32[4]{0:T(128)S(1)}, f32[64,12,512]{2,1,0:T(8,128)}, s32[4,16]{1,0:T(4,128)S(1)}, /*index=5*/f32[1...) while((s32[]{:T(128)}, f32[4,512,128]{2,1,0:T(8,128)}, ...), condition=%wide.region_5.6_spmd, body=%wide.region_2.5_spmd.sunk | while | flops 9687917568 | bytes 55387260 | solution.py:69
  197.2 0.6 dynamic_slice.61
  199.7 1.3 constant_dynamic-slice_fusion.8
  201.1 2.3 gather_fusion.3
  203.4 16.2 %fusion.106 = f32[512,16,512]{2,0,1:T(8,128)} fusion(f32[16,64,512]{2,1,0:T(8,128)S(1)} %gather_fusion.3, pred[16]{0:T(512)(128)(4,1)S(1)} %compare_and_fusion.7, f32[64,1,512]{2,1,0:T(1,128)S(1)} %constant_dynamic-slice_fusion.8, pred[]{:T(512)S(6)} %and.56), kind=kOutput, calls=%fused_computation.22.clone.1 | convolution fusion | flops 3221782528 | bytes 19005456 | tf_op jit(solution)/shard_map/cond/branch_0_fun/while/body/eval_jaxpr/dt,jds->tjs/dot_general | solution.py:9
  220.0 5.0 gather_fusion.2
  225.0 21.5 %fusion.108 = f32[4,512,128]{2,1,0:T(8,128)} fusion(f32[4,512,128]{2,1,0:T(8,128)} %get-tuple-element.303, s32[]{:T(128)} %get-tuple-element.302, f32[16,512,128]{2,1,0:T(8,128)} %gather_fusion.2, pred[16]{0:T(512)(128)(4,1)S(1)} %compare_and_fusion.7, f32[512,16,512]{2,0,1:T(8,128)} %fusion.106, f32[16,512]{1,0:T(8,128)S(1)} %multiply_reduce_fusion.5, ...), kind=kOutput, calls=%fused_computation.25.clone.1 | convolution fusion | flops 6464471040 | bytes 21269008 | tf_op jit(solution)/shard_map/cond/branch_0_fun/while/body/eval_jaxpr/tjs,jsw->tw/dot_general | solution.py:14
  246.5 0.6 dynamic_slice.61
  249.0 1.3 constant_dynamic-slice_fusion.8
  250.4 2.3 gather_fusion.3
  252.7 16.2 %fusion.106 = f32[512,16,512]{2,0,1:T(8,128)} fusion(f32[16,64,512]{2,1,0:T(8,128)S(1)} %gather_fusion.3, pred[16]{0:T(512)(128)(4,1)S(1)} %compare_and_fusion.7, f32[64,1,512]{2,1,0:T(1,128)S(1)} %constant_dynamic-slice_fusion.8, pred[]{:T(512)S(6)} %and.56), kind=kOutput, calls=%fused_computation.22.clone.1 | convolution fusion | flops 3221782528 | bytes 19005456 | tf_op jit(solution)/shard_map/cond/branch_0_fun/while/body/eval_jaxpr/dt,jds->tjs/dot_general | solution.py:9
  269.3 5.0 gather_fusion.2
  274.3 21.5 %fusion.108 = f32[4,512,128]{2,1,0:T(8,128)} fusion(f32[4,512,128]{2,1,0:T(8,128)} %get-tuple-element.303, s32[]{:T(128)} %get-tuple-element.302, f32[16,512,128]{2,1,0:T(8,128)} %gather_fusion.2, pred[16]{0:T(512)(128)(4,1)S(1)} %compare_and_fusion.7, f32[512,16,512]{2,0,1:T(8,128)} %fusion.106, f32[16,512]{1,0:T(8,128)S(1)} %multiply_reduce_fusion.5, ...), kind=kOutput, calls=%fused_computation.25.clone.1 | convolution fusion | flops 6464471040 | bytes 21269008 | tf_op jit(solution)/shard_map/cond/branch_0_fun/while/body/eval_jaxpr/tjs,jsw->tw/dot_general | solution.py:14
  298.4 1.3 constant_dynamic-slice_fusion.8
  299.8 2.3 gather_fusion.3
  302.1 16.2 %fusion.106 = f32[512,16,512]{2,0,1:T(8,128)} fusion(f32[16,64,512]{2,1,0:T(8,128)S(1)} %gather_fusion.3, pred[16]{0:T(512)(128)(4,1)S(1)} %compare_and_fusion.7, f32[64,1,512]{2,1,0:T(1,128)S(1)} %constant_dynamic-slice_fusion.8, pred[]{:T(512)S(6)} %and.56), kind=kOutput, calls=%fused_computation.22.clone.1 | convolution fusion | flops 3221782528 | bytes 19005456 | tf_op jit(solution)/shard_map/cond/branch_0_fun/while/body/eval_jaxpr/dt,jds->tjs/dot_general | solution.py:9
  318.6 5.0 gather_fusion.2
  323.6 21.5 %fusion.108 = f32[4,512,128]{2,1,0:T(8,128)} fusion(f32[4,512,128]{2,1,0:T(8,128)} %get-tuple-element.303, s32[]{:T(128)} %get-tuple-element.302, f32[16,512,128]{2,1,0:T(8,128)} %gather_fusion.2, pred[16]{0:T(512)(128)(4,1)S(1)} %compare_and_fusion.7, f32[512,16,512]{2,0,1:T(8,128)} %fusion.106, f32[16,512]{1,0:T(8,128)S(1)} %multiply_reduce_fusion.5, ...), kind=kOutput, calls=%fused_computation.25.clone.1 | convolution fusion | flops 6464471040 | bytes 21269008 | tf_op jit(solution)/shard_map/cond/branch_0_fun/while/body/eval_jaxpr/tjs,jsw->tw/dot_general | solution.py:14
  345.1 0.6 dynamic_slice.61
  347.7 1.3 constant_dynamic-slice_fusion.8
  349.1 2.3 gather_fusion.3
  351.4 16.2 %fusion.106 = f32[512,16,512]{2,0,1:T(8,128)} fusion(f32[16,64,512]{2,1,0:T(8,128)S(1)} %gather_fusion.3, pred[16]{0:T(512)(128)(4,1)S(1)} %compare_and_fusion.7, f32[64,1,512]{2,1,0:T(1,128)S(1)} %constant_dynamic-slice_fusion.8, pred[]{:T(512)S(6)} %and.56), kind=kOutput, calls=%fused_computation.22.clone.1 | convolution fusion | flops 3221782528 | bytes 19005456 | tf_op jit(solution)/shard_map/cond/branch_0_fun/while/body/eval_jaxpr/dt,jds->tjs/dot_general | solution.py:9
  367.9 5.0 gather_fusion.2
  372.9 21.5 %fusion.108 = f32[4,512,128]{2,1,0:T(8,128)} fusion(f32[4,512,128]{2,1,0:T(8,128)} %get-tuple-element.303, s32[]{:T(128)} %get-tuple-element.302, f32[16,512,128]{2,1,0:T(8,128)} %gather_fusion.2, pred[16]{0:T(512)(128)(4,1)S(1)} %compare_and_fusion.7, f32[512,16,512]{2,0,1:T(8,128)} %fusion.106, f32[16,512]{1,0:T(8,128)S(1)} %multiply_reduce_fusion.5, ...), kind=kOutput, calls=%fused_computation.25.clone.1 | convolution fusion | flops 6464471040 | bytes 21269008 | tf_op jit(solution)/shard_map/cond/branch_0_fun/while/body/eval_jaxpr/tjs,jsw->tw/dot_general | solution.py:14
  394.5 2.0 broadcast.199
  396.4 2.3 constant_dynamic-update-slice_fusion
  398.7 142.1 %all-gather.6.cloned.1.call-done = f32[48,512,128]{2,1,0:T(8,128)} async-done(((f32[12,512,128]{2,1,0:T(8,128)}), f32[48,512,128]{2,1,0:T(8,128)}) %all-gather.6.cloned.1.call-update) | async-done | bytes 12582928 | tf_op jit(solution)/shard_map/all_gather | solution.py:87
  540.9 7.6 %reduce_sum.45 = f32[12,512,128]{2,1,0:T(8,128)} reduce(f32[4,12,512,128]{3,2,1,0:T(8,128)} %bitcast.98, f32[]{:T(128)} %constant.169.clone.1), dimensions={0}, to_apply=%region_11.13 | reduce | flops 2359296 | bytes 15728644 | tf_op jit(solution)/shard_map/reduce_sum | solution.py:88
  (53 shorter events, 3.2 us)
Async XLA Ops:
  6.5 24.8 %copy-start = (f32[6144,128]{1,0:T(8,128)S(1)}, f32[6144,128]{1,0:T(8,128)}, u32[]{:S(2)}) copy-start(f32[6144,128]{1,0:T(8,128)} %param.16) | copy-start | bytes 9437188
  8.0 11.9 %all-to-all-start = ((s32[8,1,2]{2,1,0:T(1,128)}), s32[8,1,2]{2,1,0:T(1,128)S(1)}, u32[]{:S(2)}, u32[]{:S(2)}) async-start(s32[8,1,2]{2,1,0:T(1,128)} %copy.24), calls=%async_computation | async-start | bytes 8192 | tf_op jit(solution)/shard_map/all_to_all | solution.py:32
  27.0 53.4 %all-to-all-start.1 = ((f32[8,2,64,512]{3,2,1,0:T(8,128)}), f32[8,2,64,512]{3,2,1,0:T(8,128)}, u32[]{:S(2)}, u32[]{:S(2)}) async-start(f32[8,2,64,512]{3,2,1,0:T(8,128)} %broadcast_select_fusion.1), calls=%async_computation.1 | async-start | bytes 4194304 | tf_op jit(solution)/shard_map/all_to_all | solution.py:35
  80.4 116.1 %all-to-all-start.2 = ((f32[8,2,512,128]{3,2,1,0:T(8,128)}), f32[8,2,512,128]{3,2,1,0:T(8,128)}, u32[]{:S(2)}, u32[]{:S(2)}) async-start(f32[8,2,512,128]{3,2,1,0:T(8,128)} %broadcast_select_fusion), calls=%async_computation.2 | async-start | bytes 8388608 | tf_op jit(solution)/shard_map/all_to_all | solution.py:36
  85.0 47.3 %all-reduce.2.cloned.1.call-start = ((), (), s32[]{:S(2)}) async-start(), calls=%async_computation.3 | async-start | bytes 262144 | tf_op jit(solution)/shard_map/psum | solution.py:50
  88.5 46.7 %copy-start.3 = (f32[64,6144]{1,0:T(8,128)S(1)}, f32[64,6144]{1,0:T(8,128)}, u32[]{:S(2)}) copy-start(f32[64,6144]{1,0:T(8,128)} %param.15) | copy-start | bytes 4718596
  88.5 107.9 %all-gather.4.cloned.1.call-start = ((), (), s32[]{:S(2)}) async-start(), calls=%async_computation.4 | async-start | bytes 1179648 | tf_op jit(solution)/shard_map/all_gather | solution.py:53
  132.3 5.2 copy-start.5
  132.3 64.1 %copy-start.4 = (s32[12,8]{0,1:T(8,128)S(1)}, s32[12,8]{0,1:T(8,128)}, u32[]{:S(2)}) copy-start(s32[12,8]{0,1:T(8,128)} %param.20) | copy-start | bytes 1156
  132.3 408.5 %all-gather.6.cloned.1.call-start = ((), (), s32[]{:S(2)}) async-start(), calls=%async_computation.5 | async-start | bytes 15728640 | tf_op jit(solution)/shard_map/all_gather | solution.py:87
  540.9 7.6 %copy-start.1 = (f32[6144,128]{1,0:T(8,128)S(1)}, f32[6144,128]{1,0:T(8,128)}, u32[]{:S(2)}) copy-start(f32[6144,128]{1,0:T(8,128)} %param.16) | copy-start | bytes 9437188
Sparse Core Ops, SparseCore 0:
  88.7 43.5 all-reduce.1
  133.9 39.0 all-gather.3
  398.8 141.9 all-gather.5
